TPU v7x, 32 devices: a whole 2x2x4 slice. The times are simulated.
32 devices in a mesh: group: 2 (over y), context: 4 (over z), head: 4 (over x, core).
Axes of the slice: x: 2, y: 2, z: 4, core: 2. Of those that a mesh axis runs over, the one named last changes fastest.
Arguments:
- dn_query: bfloat16 [1024, 2048], P(('group', 'context'), 'head'), parts along dimension 0, may hold values from -6 to 6
- dn_key: bfloat16 [1024, 2048], P(('group', 'context'), 'head'), parts along dimension 0, may hold values from -6 to 6
- dn_value: bfloat16 [1024, 4096], P(('group', 'context'), 'head'), parts along dimension 0, may hold values from -6 to 6
- dn_gate: bfloat16 [1024, 4096], P(('group', 'context'), 'head'), parts along dimension 0, may hold values from -6 to 6
- dn_beta_logit: float32 [1024, 32], P(('group', 'context'), 'head'), parts along dimension 0, may hold values from -6 to 6
- dn_decay: float32 [1024, 32], P(('group', 'context'), 'head'), parts along dimension 0, may hold values from -1 to 0
- dn_norm_gain: float32 [128], replicated, may hold values from 0.1 to 1.9
- prefix_state: bfloat16 [4, 32, 128, 128], P('group', 'head', 'context'), parts along dimension 0, may hold values from -6 to 6
- at_query: bfloat16 [1024, 4096], P(('group', 'context'), 'head'), parts along dimension 0, may hold values from -6 to 6
- at_gate: bfloat16 [1024, 4096], P(('group', 'context'), 'head'), parts along dimension 0, may hold values from -6 to 6
- at_key: bfloat16 [1024, 512], P(('group', 'context')), parts along dimension 0, may hold values from -6 to 6
- at_value: bfloat16 [1024, 512], P(('group', 'context')), parts along dimension 0, may hold values from -6 to 6
- prefix_key: bfloat16 [16, 64, 512], P(('group', 'context')), parts along dimension 0, may hold values from -6 to 6
- prefix_value: bfloat16 [16, 64, 512], P(('group', 'context')), parts along dimension 0, may hold values from -6 to 6
- req_len: int32 [8], P('group'), parts along dimension 0, may hold values from 1 to 256, 512 in all
- req_prefix: int32 [8], P('group'), parts along dimension 0, may hold values from 0 to 1, as said below
- req_offset: int32 [8], P('group'), parts along dimension 0, may hold values from 64 to 256, as said below
- block_table: int32 [16], P('group'), parts along dimension 0, may hold values from 0 to 7, each once
Outputs:
- dn_out: bfloat16 [1024, 4096], P(('group', 'context'), 'head'), parts along dimension 0
- at_out: bfloat16 [1024, 4096], P(('group', 'context'), 'head'), parts along dimension 0
There are 2 independent parts, one for each index of `group`. A program takes and returns all parts, laid end to end along the dimension named above; an argument that names none is the same for every part. Nothing has to cross between parts.
Inputs may be any that keep to these rules, and one draw needn't show every extreme that they name: `req_len`: requests lie one after another in row order; the longest has exactly 256 new tokens. `req_prefix`: every prefix is extended by one or more requests. `req_offset`: equal for the requests of one prefix: the number of its cached positions; one prefix holds 256, another from a quarter to a half of 256. `block_table`: entry p * 4 + j is the slot of block j of prefix p; every slot once.
All inputs are finite; a program needn't handle non-finite values.
Results may differ from a plain program's by a relative error of at most 0.011.
Values may be sent and summed in bfloat16 or wider, within the bound.
A program may use at most 128 MiB of HBM per device.

v0:
```python
import math
import jax
import jax.numpy as jnp
from jax import lax
from jax.sharding import PartitionSpec as P

VH = 32
KH = 16
DK = 128
DV = 128
HQ = 16
KVH = 2
HD = 256
ROT = 64
ROPE_THETA = 10000000.0
YARN_FACTOR = 4.0
YARN_ANCHOR = 262144.0
NEG_LARGE = -1e30
HIGH = lax.Precision.HIGHEST


def carried_in(x, axis, join, neutral):
    place = lax.axis_index(axis)
    gathered = jax.tree.map(
        lambda a, kind: lax.all_gather(a.astype(kind), axis),
        x,
        (jnp.bfloat16, jnp.bfloat16, jnp.bfloat16),
    )
    state = jax.tree.map(lambda a, e: jnp.zeros_like(a) + jnp.asarray(e, a.dtype), x, neutral)

    def one(turn, state):
        return join(
            state,
            jax.tree.map(
                lambda a, own: lax.dynamic_index_in_dim(a, turn, 0, False).astype(own.dtype),
                gathered,
                x,
            ),
        )

    return lax.fori_loop(0, place, one, state)


def yarn_tables(positions, rotary):
    half = rotary // 2
    log_theta = math.log(ROPE_THETA)
    lower = max(
        math.floor(rotary * math.log(YARN_ANCHOR / (64.0 * math.pi)) / (2.0 * log_theta)), 0
    )
    upper = min(
        math.ceil(rotary * math.log(YARN_ANCHOR / (2.0 * math.pi)) / (2.0 * log_theta)), rotary - 1
    )
    spread = float(upper - lower)
    index = jnp.arange(half, dtype=jnp.float32)
    plain_frequency = jnp.exp(index * (-2.0 * log_theta / rotary))
    keep = 1.0 - jnp.clip((index - lower) / spread, 0.0, 1.0)
    frequency = plain_frequency * keep + plain_frequency / YARN_FACTOR * (1.0 - keep)
    angles = positions.astype(jnp.float32)[:, None] * frequency[None, :]
    attention_factor = 0.1 * math.log(YARN_FACTOR) + 1.0
    return (jnp.cos(angles) * attention_factor, jnp.sin(angles) * attention_factor)


def rotate(values, cosines, sines, rotary):
    half = rotary // 2
    first = values[..., :half]
    second = values[..., half:rotary]
    cosines = cosines[:, None, :]
    sines = sines[:, None, :]
    return jnp.concatenate(
        [first * cosines - second * sines, second * cosines + first * sines, values[..., rotary:]],
        axis=-1,
    )


def unit_rows(values):
    return values * lax.rsqrt(jnp.sum(values * values, axis=-1, keepdims=True) + 1e-06)


def row_layout(rows, req_len, req_prefix, req_offset):
    starts = jnp.cumsum(req_len) - req_len
    leading_found = (starts[None, :] <= rows[:, None]).astype(jnp.int32)
    segment = jnp.sum(leading_found, axis=1) - 1
    choose = (segment[:, None] == jnp.arange(req_len.shape[0], dtype=jnp.int32)[None, :]).astype(
        jnp.int32
    )
    first = jnp.sum(choose * starts[None, :], axis=1)
    prefix = jnp.sum(choose * req_prefix[None, :], axis=1)
    offset = jnp.sum(choose * req_offset[None, :], axis=1)
    return (segment, first, prefix, offset, offset + rows - first)


def absorb(state, queries, search_handles, values, visible):
    peak, total, summed = state
    scores = jnp.einsum(
        "thd,nd->thn", queries, search_handles, preferred_element_type=jnp.float32
    ) * search_handles.shape[-1] ** (-0.5)
    seen = visible[:, None, :]
    scores = jnp.where(seen, scores, NEG_LARGE)
    new_peak = jnp.maximum(peak, jnp.max(scores, axis=-1))
    weights = jnp.where(seen, jnp.exp(scores - new_peak[..., None]), 0.0)
    shrink = jnp.exp(peak - new_peak)
    total = total * shrink + jnp.sum(weights, axis=-1)
    summed = summed * shrink[..., None] + jnp.einsum(
        "thn,nd->thd", weights.astype(jnp.bfloat16), values, preferred_element_type=jnp.float32
    )
    return (new_peak, total, summed)


def compose(earlier, later):
    map_early, add_early, flag_early = earlier
    map_late, add_late, flag_late = later
    fresh = flag_late > 0.5
    joined_map = jnp.where(
        fresh, map_late, jnp.einsum("hij,hjk->hik", map_early, map_late, precision=HIGH)
    )
    joined_add = jnp.where(
        fresh, add_late, jnp.einsum("hvj,hjk->hvk", add_early, map_late, precision=HIGH) + add_late
    )
    return (joined_map, joined_add, jnp.maximum(flag_early, flag_late))


def shards(
    dn_query,
    dn_key,
    dn_value,
    dn_gate,
    dn_beta_logit,
    dn_decay,
    dn_norm_gain,
    prefix_state,
    at_query,
    at_gate,
    at_key,
    at_value,
    prefix_key,
    prefix_value,
    req_len,
    req_prefix,
    req_offset,
    block_table,
):
    tokens_here = dn_query.shape[0]
    key_heads = dn_query.shape[1] // DK
    value_heads = dn_value.shape[1] // DV
    query_heads = at_query.shape[1] // HD
    device = lax.axis_index("context")
    row_start = device * tokens_here
    rows = row_start + jnp.arange(tokens_here, dtype=jnp.int32)
    segment, first, prefix, offset, position = row_layout(rows, req_len, req_prefix, req_offset)
    query = jnp.repeat(
        unit_rows(dn_query.reshape(tokens_here, key_heads, DK).astype(jnp.float32)) * DK ** (-0.5),
        VH // KH,
        axis=1,
    )
    key = jnp.repeat(
        unit_rows(dn_key.reshape(tokens_here, key_heads, DK).astype(jnp.float32)), VH // KH, axis=1
    )
    query_heads_first = jnp.transpose(query, (1, 0, 2))
    key_heads_first = jnp.transpose(key, (1, 0, 2))
    value_heads_first = jnp.transpose(
        dn_value.reshape(tokens_here, value_heads, DV).astype(jnp.float32), (1, 0, 2)
    )
    beta = jax.nn.sigmoid(dn_beta_logit).T
    same = segment[:, None] == segment[None, :]
    causal = same & (rows[:, None] >= rows[None, :])
    strict = same & (rows[:, None] > rows[None, :])
    running = jnp.dot(causal.astype(jnp.float32), dn_decay, precision=HIGH).T
    gaps = running[:, :, None] - running[:, None, :]
    decay_mat = jnp.where(causal[None], jnp.exp(jnp.where(causal[None], gaps, 0.0)), 0.0)
    key_gram = jnp.einsum("hid,hjd->hij", key_heads_first, key_heads_first, precision=HIGH)
    query_key = jnp.einsum("hid,hjd->hij", query_heads_first, key_heads_first, precision=HIGH)
    lower_mat = jnp.where(strict[None], beta[:, :, None] * key_gram * decay_mat, 0.0)
    system = jnp.eye(tokens_here, dtype=jnp.float32)[None] + lower_mat
    start_decay = jnp.exp(running)
    solve_values = beta[:, :, None] * value_heads_first
    solve_keys = (beta * start_decay)[:, :, None] * key_heads_first
    solved = jax.scipy.linalg.solve_triangular(
        system, jnp.concatenate([solve_values, solve_keys], axis=2), lower=True, unit_diagonal=True
    )
    update = solved[:, :, :DV]
    wy_keys = solved[:, :, DV:]
    mixing = decay_mat * query_key
    local_out = jnp.einsum("hij,hjv->hiv", mixing, update, precision=HIGH)
    reach = start_decay[:, :, None] * query_heads_first - jnp.einsum(
        "hij,hjk->hik", mixing, wy_keys, precision=HIGH
    )
    tail = segment == segment[tokens_here - 1]
    end_gaps = running[:, tokens_here - 1 : tokens_here] - running
    end_weight = jnp.where(tail[None, :], jnp.exp(jnp.where(tail[None, :], end_gaps, 0.0)), 0.0)
    end_decay = start_decay[:, tokens_here - 1]
    identity_mat = jnp.eye(DK, dtype=jnp.float32)
    carry_map = end_decay[:, None, None] * identity_mat[None] - jnp.einsum(
        "hjk,hj,hjl->hkl", wy_keys, end_weight, key_heads_first, precision=HIGH
    )
    carry_add = jnp.einsum("hjv,hj,hjl->hvl", update, end_weight, key_heads_first, precision=HIGH)
    restart = (first[tokens_here - 1] >= row_start).astype(jnp.float32)
    identity = (
        jnp.broadcast_to(identity_mat, (value_heads, DK, DK)),
        jnp.zeros((value_heads, DV, DK), jnp.float32),
        jnp.zeros((), jnp.float32),
    )
    into_map, into_add, into_flag = carried_in(
        (carry_map, carry_add, restart), "context", compose, identity
    )
    carried = ((segment == segment[0]) & (first[0] < row_start))[None, :, None]
    through = jnp.einsum("hkl,hil->hik", into_map, reach, precision=HIGH)
    extra = jnp.einsum("hvk,hik->hiv", into_add, reach, precision=HIGH)
    weight_vec = jnp.where(carried, through, reach).astype(jnp.bfloat16)
    core = local_out + jnp.where(carried, extra, 0.0)
    owner_ids = jnp.arange(prefix_state.shape[0], dtype=jnp.int32)
    select = (prefix[None, :] == owner_ids[:, None]).astype(jnp.bfloat16)
    masked = select[:, None, :, None] * weight_vec[None]
    state_part = jnp.einsum(
        "phik,phvk->hiv",
        masked,
        lax.all_gather(prefix_state, "context", axis=2, tiled=True),
        preferred_element_type=jnp.float32,
    )
    core = core + state_part
    core_rows = jnp.transpose(core, (1, 0, 2))
    normed = core_rows * lax.rsqrt(jnp.mean(core_rows * core_rows, axis=-1, keepdims=True) + 1e-06)
    gate_rows = dn_gate.reshape(tokens_here, value_heads, DV).astype(jnp.float32)
    dn_out = (
        (normed * dn_norm_gain * jax.nn.silu(gate_rows))
        .reshape(tokens_here, value_heads * DV)
        .astype(jnp.bfloat16)
    )
    group = HQ // KVH
    kv_head = lax.axis_index("head") * query_heads // group
    cosines, sines = yarn_tables(position, ROT)
    query_rot = rotate(
        at_query.reshape(tokens_here, query_heads, HD).astype(jnp.float32), cosines, sines, ROT
    ).astype(jnp.bfloat16)
    new_key = lax.dynamic_slice_in_dim(at_key, kv_head * HD, HD, 1).reshape(tokens_here, 1, HD)
    new_key = (
        rotate(new_key.astype(jnp.float32), cosines, sines, ROT)
        .reshape(tokens_here, HD)
        .astype(jnp.bfloat16)
    )
    new_value = lax.dynamic_slice_in_dim(at_value, kv_head * HD, HD, 1)
    cached_key = lax.dynamic_slice_in_dim(prefix_key, kv_head * HD, HD, 2)
    cached_value = lax.dynamic_slice_in_dim(prefix_value, kv_head * HD, HD, 2)
    table_index = jnp.arange(block_table.shape[0], dtype=jnp.int32)
    blocks_per_prefix = block_table.shape[0] // prefix_state.shape[0]
    state = (
        jnp.full((tokens_here, query_heads), NEG_LARGE, jnp.float32),
        jnp.zeros((tokens_here, query_heads), jnp.float32),
        jnp.zeros((tokens_here, query_heads, HD), jnp.float32),
    )
    search_handles = lax.all_gather(cached_key, "context", axis=0, tiled=True)
    values = lax.all_gather(cached_value, "context", axis=0, tiled=True)
    count = search_handles.shape[0]
    width = search_handles.shape[1]
    slots = jnp.arange(count, dtype=jnp.int32)
    entry = jnp.sum(
        jnp.where(block_table[None, :] == slots[:, None], table_index[None, :], 0), axis=1
    )
    owner = jnp.repeat(entry // blocks_per_prefix, width)
    where_in = (
        (entry % blocks_per_prefix)[:, None] * width + jnp.arange(width, dtype=jnp.int32)[None, :]
    ).reshape(count * width)
    visible = (owner[None, :] == prefix[:, None]) & (where_in[None, :] < offset[:, None])
    flat_keys = search_handles.reshape(count * width, search_handles.shape[2])
    flat_values = values.reshape(count * width, values.shape[2])
    state = absorb(state, query_rot, flat_keys, flat_values, visible)
    search_handles = lax.all_gather(new_key, "context", axis=0, tiled=True)
    values = lax.all_gather(new_value, "context", axis=0, tiled=True)
    key_rows = jnp.arange(search_handles.shape[0], dtype=jnp.int32)
    key_segment = row_layout(key_rows, req_len, req_prefix, req_offset)[0]
    visible = (key_segment[None, :] == segment[:, None]) & (key_rows[None, :] <= rows[:, None])
    state = absorb(state, query_rot, search_handles, values, visible)
    peak, total, summed = state
    attention = summed / total[..., None]
    gate_att = at_gate.reshape(tokens_here, query_heads, HD).astype(jnp.float32)
    at_out = (
        (attention * jax.nn.sigmoid(gate_att))
        .reshape(tokens_here, query_heads * HD)
        .astype(jnp.bfloat16)
    )
    return (dn_out, at_out)


def solution(mesh):
    placed = (
        P(("group", "context"), "head"),
        P(("group", "context"), "head"),
        P(("group", "context"), "head"),
        P(("group", "context"), "head"),
        P(("group", "context"), "head"),
        P(("group", "context"), "head"),
        P(),
        P("group", "head", "context", None),
        P(("group", "context"), "head"),
        P(("group", "context"), "head"),
        P(("group", "context"), None),
        P(("group", "context"), None),
        P(("group", "context"), None, None),
        P(("group", "context"), None, None),
        P("group"),
        P("group"),
        P("group"),
        P("group"),
    )
    return jax.shard_map(
        shards,
        mesh=mesh,
        in_specs=placed,
        out_specs=(P(("group", "context"), "head"), P(("group", "context"), "head")),
        check_vma=False,
    )
```

profile of v0, /device:TPU:26, one launch (start us, length us, event | category | flops | bytes accessed | tf_op | source)
XLA Modules:
  0.0 243.3 jit_solution(15976261732324481945)
XLA Ops:
  7.3 0.7 copy-done.35
  8.3 0.7 fusion.73
  9.1 0.7 fusion.74
  11.4 0.6 copy-done.25
  12.8 2.1 fusion.15
  14.9 79.4 %custom-call.4 = f32[8,1,128,128]{2,3,1,0:T(8,128)S(1)} custom-call(f32[8,1,128,128]{3,2,1,0:T(8,128)} %fusion.15), custom_call_target="InvertDiagBlocksLowerTriangular" | custom-call | tf_op jit(solution)/shard_map/jit(_solve_triangular)/vmap()/triangular_solve | solution.py:177
  94.3 1.8 compare_and_fusion.3
  96.2 0.5 bitcast_multiply_fusion.1
  96.7 1.0 fusion.22
  97.8 1.7 convolution_convert_fusion
  99.8 1.7 fusion.20
  101.6 0.8 copy-done.11
  102.8 0.8 slice.68
  104.2 16.7 %all-gather.2 = bf16[512,1,256]{0,2,1:T(8,128)(2,1)} all-gather(bf16[128,1,256]{0,2,1:T(8,128)(2,1)S(1)} %pad_maximum_fusion.1), channel_id=4, replica_groups=mesh['group'=2,'context'=4,'head'=4] {'context'}, dimensions={0}, use_global_device_ids=true | all-gather | bytes 327680 | tf_op jit(solution)/shard_map/all_gather | solution.py:266
  121.1 0.7 fusion.49
  121.9 16.6 %all_gather.40 = bf16[8,64,256]{2,1,0:T(8,128)(2,1)} all-gather(bf16[2,64,256]{2,1,0:T(8,128)(2,1)S(1)} %constant_dynamic-slice_fusion.3), channel_id=1, replica_groups=mesh['group'=2,'context'=4,'head'=4] {'context'}, dimensions={0}, use_global_device_ids=true | all-gather | bytes 327680 | tf_op jit(solution)/shard_map/all_gather | solution.py:250
  138.9 16.8 %all_gather.41 = bf16[8,64,256]{2,1,0:T(8,128)(2,1)} all-gather(bf16[2,64,256]{2,1,0:T(8,128)(2,1)S(1)} %constant_dynamic-slice_fusion.2), channel_id=1, replica_groups=mesh['group'=2,'context'=4,'head'=4] {'context'}, dimensions={0}, use_global_device_ids=true | all-gather | bytes 327680 | tf_op jit(solution)/shard_map/all_gather | solution.py:251
  155.7 16.5 %all_gather.43 = bf16[512,256]{1,0:T(8,128)(2,1)} all-gather(bf16[128,256]{1,0:T(8,128)(2,1)S(1)} %constant_dynamic-slice_fusion.4), channel_id=1, replica_groups=mesh['group'=2,'context'=4,'head'=4] {'context'}, dimensions={0}, use_global_device_ids=true | all-gather | bytes 327680 | tf_op jit(solution)/shard_map/all_gather | solution.py:267
  172.5 1.0 copy.164
  173.6 0.8 multiply_reduce_fusion.2
  175.5 0.6 copy-done.5
  176.2 0.5 fusion.76
  176.7 0.5 copy-done.7
  177.2 0.5 fusion.75
  177.7 0.5 copy-done.26
  178.2 0.7 fusion.26
  178.9 0.6 multiply_add_fusion
  179.5 0.6 dynamic-slice
  180.1 1.2 fusion.18
  181.3 0.5 broadcast.492
  181.8 1.9 dynamic-update-slice
  183.7 2.3 fusion.19
  186.0 0.6 copy-done.39
  186.6 8.6 %all-reduce = bf16[4]{0:T(256)(128)(2,1)} all-reduce(bf16[4]{0:T(256)(128)(2,1)S(1)} %copy-done.39), channel_id=1, replica_groups=mesh['group'=2,'context'=4,'head'=4] {'context'}, use_global_device_ids=true, to_apply=%add | all-reduce | flops 4 | bytes 16
  195.3 1.1 copy.165
  196.4 0.9 copy.167
  197.5 0.9 copy-done.17
  198.4 0.9 copy-done.13
  199.7 15.1 %all_gather.39 = bf16[2,8,128,128]{3,2,0,1:T(8,128)(2,1)S(1)} all-gather(bf16[2,8,32,128]{3,2,0,1:T(8,128)(2,1)S(1)} %copy.150), channel_id=1, replica_groups=mesh['group'=2,'context'=4,'head'=4] {'context'}, dimensions={2}, use_global_device_ids=true | all-gather | bytes 655360 | tf_op jit(solution)/shard_map/all_gather | solution.py:216
  214.8 0.6 compare_convert_fusion
  215.5 0.6 copy-done.19
  216.1 1.2 convolution_multiply_fusion.3
  217.3 1.5 fusion.43
  218.8 0.7 convolution_subtract_fusion.1
  219.6 0.5 copy-done.38
  220.2 11.2 %while.14 = (s32[]{:T(128)}, f32[8,128,128]{1,2,0:T(8,128)S(1)}, f32[8,128,128]{1,2,0:T(8,128)S(1)}, s32[]{:T(128)}, bf16[4]{0:T(256)(128)(2,1)S(1)}, /*index=5*...) while((s32[]{:T(128)}, f32[8,128,128]{1,2,0:T(8,128)S(1)}, ...), condition=%wide.region_6.7_spmd, body=%wide.region_5.6_spmd.sunk | while | flops 403308544 | bytes 7340196 | solution.py:41
  220.2 1.1 constant_dynamic-slice_fusion.7
  221.4 0.6 dynamic_slice.39
  222.7 0.5 fusion.106
  223.4 0.5 fusion.105
  223.9 1.1 constant_dynamic-slice_fusion.7
  225.2 0.6 dynamic_slice.39
  226.5 0.5 fusion.106
  227.2 0.5 fusion.105
  227.7 1.1 constant_dynamic-slice_fusion.7
  228.9 0.6 dynamic_slice.39
  230.2 0.5 fusion.106
  230.9 0.5 fusion.105
  231.4 0.6 copy-done.27
  232.0 0.7 fusion.21
  233.0 0.7 copy-done.1
  233.7 0.8 multiply_reduce_fusion
  234.6 0.6 copy-done.30
  235.6 0.9 copy.166
  (151 shorter events, 7.8 us)
Async XLA Ops:
  7.2 96.5 %copy-start = (bf16[128,512]{1,0:T(8,128)(2,1)S(1)}, bf16[128,512]{1,0:T(8,128)(2,1)}, u32[]{:S(2)}) copy-start(bf16[128,512]{1,0:T(8,128)(2,1)} %param.30) | copy-start | bytes 393220
  7.2 212.3 %all-gather.8.cloned.1.call-start = ((), (), s32[]{:S(2)}) async-start(), calls=%async_computation.1 | async-start | bytes 1310720 | tf_op jit(solution)/shard_map/all_gather | solution.py:25
  7.2 3.6 %copy-start.15 = (bf16[128,512]{1,0:T(8,128)(2,1)S(1)}, bf16[128,512]{1,0:T(8,128)(2,1)}, u32[]{:S(2)}) copy-start(bf16[128,512]{1,0:T(8,128)(2,1)} %param.21) | copy-start | bytes 393220
  7.3 92.5 %copy-start.2 = (f32[128,128]{1,0:T(8,128)}, f32[128,128]{1,0:T(8,128)S(1)}, u32[]{:S(2)}) copy-start(f32[128,128]{1,0:T(8,128)S(1)} %get-tuple-element.158) | copy-start | bytes 196612
  7.3 0.7 copy-start.35
  8.3 0.7 copy-start.32
  8.3 0.7 copy-start.33
  9.0 166.3 %copy-start.28 = (s32[128]{0:T(128)}, s32[128]{0:T(128)S(1)}, u32[]{:S(2)}) copy-start(s32[128]{0:T(128)S(1)} %get-tuple-element.108) | copy-start | bytes 1540
  9.0 1.3 copy-start.34
  10.6 85.6 %copy-start.18 = (f32[8,128]{1,0:T(8,128)}, f32[8,128]{1,0:T(8,128)S(1)}, u32[]{:S(2)}) copy-start(f32[8,128]{1,0:T(8,128)S(1)} %convolution_bitcast_fusion.3) | copy-start | bytes 12292
  11.4 0.7 copy-start.25
  11.4 1.0 copy-start.10
  96.2 3.4 %copy-start.20 = (f32[8,128]{1,0:T(8,128)}, f32[8,128]{1,0:T(8,128)S(1)}, u32[]{:S(2)}) copy-start(f32[8,128]{1,0:T(8,128)S(1)} %get-tuple-element.135) | copy-start | bytes 12292
  99.5 120.0 %all-gather.6.cloned.1.call-start = ((), (), s32[]{:S(2)}) async-start(), calls=%async_computation | async-start | bytes 1310720 | tf_op jit(solution)/shard_map/all_gather | solution.py:25
  101.5 0.9 copy-start.11
  120.9 1.0 copy-start.22
  121.9 16.6 %copy-start.36 = (s32[8]{0:T(128)S(1)}, s32[8]{0:T(128)}, u32[]{:S(2)}) copy-start(s32[8]{0:T(128)} %param.37) | copy-start | bytes 100
  121.9 17.0 %copy-start.23 = (bf16[2,64,512]{2,1,0:T(8,128)(2,1)S(1)}, bf16[2,64,512]{2,1,0:T(8,128)(2,1)}, u32[]{:S(2)}) copy-start(bf16[2,64,512]{2,1,0:T(8,128)(2,1)} %param.33) | copy-start | bytes 393220
  138.9 16.8 %copy-start.24 = (bf16[128,512]{1,0:T(8,128)(2,1)S(1)}, bf16[128,512]{1,0:T(8,128)(2,1)}, u32[]{:S(2)}) copy-start(bf16[128,512]{1,0:T(8,128)(2,1)} %param.31) | copy-start | bytes 393220
  155.7 16.5 %copy-start.12 = (bf16[128,1024]{1,0:T(8,128)(2,1)S(1)}, bf16[128,1024]{1,0:T(8,128)(2,1)}, u32[]{:S(2)}) copy-start(bf16[128,1024]{1,0:T(8,128)(2,1)} %param.29) | copy-start | bytes 786436
  172.5 1.0 copy-start.16
  175.2 1.0 copy-start.5
  175.2 1.0 copy-start.14
  175.3 0.9 copy-start.8
  176.2 0.9 copy-start.7
  177.7 0.6 copy-start.26
  178.2 1.9 copy-start.6
  178.9 0.7 copy-start.37
  180.1 3.6 %copy-start.4 = (f32[128,4,256]{2,0,1:T(8,128)S(1)}, f32[128,4,256]{2,0,1:T(8,128)}, u32[]{:S(2)}) copy-start(f32[128,4,256]{2,0,1:T(8,128)} %copy.164) | copy-start | bytes 1572868
  183.7 2.3 copy-start.9
  186.0 0.6 copy-start.39
  186.0 9.2 %copy-start.3 = (f32[128,128]{1,0:T(8,128)S(1)}, f32[128,128]{1,0:T(8,128)}, u32[]{:S(2)}) copy-start(f32[128,128]{1,0:T(8,128)} %copy-done.2) | copy-start | bytes 196612
  197.5 0.9 copy-start.17
  198.4 0.9 copy-start.13
  199.7 15.2 %copy-start.29 = (s32[128]{0:T(128)S(1)}, s32[128]{0:T(128)}, u32[]{:S(2)}) copy-start(s32[128]{0:T(128)} %copy-done.28) | copy-start | bytes 1540
  215.4 0.7 copy-start.19
  217.3 1.5 copy-start.21
  219.6 0.6 copy-start.38
  231.4 0.6 copy-start.27
  232.0 0.7 copy-start.31
  232.7 1.0 copy-start.1
  234.5 0.7 copy-start.30
Sparse Core Ops, SparseCore 0:
  99.7 32.8 all-gather.7
  134.7 33.2 all-gather.5
where the time goes:
time: 244 us; the launch traced here: 243 us
  blocking collectives  90.3 us (37%)
  other arithmetic  87.6 us (36%)
  local copies, waits for them, and re-layouts  27.8 us (11%)
  matrix products  19.2 us (8%)
  between operations  16.1 us (7%)
    another operation x2, other arithmetic, shards(): jax.scipy.linalg.solve_triangular(system, jnp.concatenate([solve_values,...  79.4 us
    all_gather x1, blocking collectives, shards(): values = lax.all_gather(cached_value, 'context', axis=0, tiled=True)  16.8 us
    all_gather x1, blocking collectives, shards(): search_handles = lax.all_gather(new_key, 'context', axis=0, tiled=True)  16.7 us
    all_gather x1, blocking collectives, shards(): search_handles = lax.all_gather(cached_key, 'context', axis=0, tiled=True)  16.6 us
    all_gather x1, blocking collectives, shards(): values = lax.all_gather(new_value, 'context', axis=0, tiled=True)  16.5 us
    unnamed x91, local copies, waits for them, and re-layouts  15.3 us
    all_gather x1, blocking collectives, shards(): lax.all_gather(prefix_state, 'context', axis=2, tiled=True)  15.1 us
    unnamed x1, blocking collectives  8.58 us
  transfers between devices with their start and end apart: 2, of which 0 were waited for; matrix products, arithmetic and copies ran while one was open for 9% of the time, Pallas kernels for 0%

commit v1 on v0

--- a/solution.py
+++ b/solution.py
@@ -17,6 +17,14 @@
 YARN_ANCHOR = 262144.0
 NEG_LARGE = -1e30
 HIGH = lax.Precision.HIGHEST
+
+
+def proceed_boxes(obj, u_in):
+    return jnp.split(
+        lax.all_gather(jnp.concatenate([obj, u_in], axis=1), "context", axis=0, tiled=True),
+        [obj.shape[1]],
+        axis=1,
+    )
 
 
 def carried_in(x, axis, join, neutral):
@@ -263,8 +271,7 @@
     flat_keys = search_handles.reshape(count * width, search_handles.shape[2])
     flat_values = values.reshape(count * width, values.shape[2])
     state = absorb(state, query_rot, flat_keys, flat_values, visible)
-    search_handles = lax.all_gather(new_key, "context", axis=0, tiled=True)
-    values = lax.all_gather(new_value, "context", axis=0, tiled=True)
+    search_handles, values = proceed_boxes(new_key, new_value)
     key_rows = jnp.arange(search_handles.shape[0], dtype=jnp.int32)
     key_segment = row_layout(key_rows, req_len, req_prefix, req_offset)[0]
     visible = (key_segment[None, :] == segment[:, None]) & (key_rows[None, :] <= rows[:, None])

time: 244 us -> 229 us (0.939)
  blocking collectives: 90.3 us -> 81.3 us
  matrix products: 19.2 us -> 15.6 us
    all_gather x2 -> x1, blocking collectives: 33.2 us -> 26.4 us  [proceed_boxes(): lax.all_gather(jnp.concatenate([obj, u_in], axis=1), 'context', axis=0, t...]
    dot_general x2, matrix products: 3.44 us -> 0.73 us  [absorb(): jnp.einsum('thn,nd->thd', weights.astype(jnp.bfloat16), values, preferred...]
    unnamed x91 -> x88, local copies, waits for them, and re-layouts: 15.3 us -> 14 us
  transfers between devices with their start and end apart: 2 -> 2, of which waited for: 0 -> 0; matrix products, arithmetic and copies ran while one was open for 9% -> 8% of each run, Pallas kernels for 0% -> 0%
where the time goes in v1:
time: 229 us; the launch traced here: 228 us
  other arithmetic  86.2 us (38%)
  blocking collectives  81.3 us (36%)
  local copies, waits for them, and re-layouts  26.6 us (12%)
  between operations  16.1 us (7%)
  matrix products  15.6 us (7%)
    another operation x2, other arithmetic, shards(): jax.scipy.linalg.solve_triangular(system, jnp.concatenate([solve_values,...  78.6 us
    all_gather x1, blocking collectives, proceed_boxes(): lax.all_gather(jnp.concatenate([obj, u_in], axis=1), 'context', axis=0, t...  26.4 us
    all_gather x1, blocking collectives, shards(): values = lax.all_gather(cached_value, 'context', axis=0, tiled=True)  16.1 us
    all_gather x1, blocking collectives, shards(): lax.all_gather(prefix_state, 'context', axis=2, tiled=True)  15.1 us
    all_gather x1, blocking collectives, shards(): search_handles = lax.all_gather(cached_key, 'context', axis=0, tiled=True)  15 us
    unnamed x88, local copies, waits for them, and re-layouts  14 us
    unnamed x1, blocking collectives  8.71 us
    dynamic_slice x12, local copies, waits for them, and re-layouts, one(): lax.dynamic_index_in_dim(a, turn, 0, False).astype(own.dtype)  6.04 us
  transfers between devices with their start and end apart: 2, of which 0 were waited for; matrix products, arithmetic and copies ran while one was open for 8% of the time, Pallas kernels for 0%

profile of v1, /device:TPU:26, one launch (start us, length us, event | category | flops | bytes accessed | tf_op | source)
XLA Modules:
  0.0 228.1 jit_solution(6046770942358816804)
XLA Ops:
  7.3 0.7 copy-done.34
  8.3 0.6 fusion.71
  8.9 0.7 select_reduce_fusion.1
  9.6 0.6 fusion.72
  11.8 0.6 copy-done.21
  13.3 1.3 fusion.15
  14.6 78.6 %custom-call.4 = f32[8,1,128,128]{2,3,1,0:T(8,128)S(1)} custom-call(f32[8,1,128,128]{3,2,1,0:T(8,128)S(1)} %fusion.15), custom_call_target="InvertDiagBlocksLowerTriangular" | custom-call | tf_op jit(solution)/shard_map/jit(_solve_triangular)/vmap()/triangular_solve | solution.py:185
  93.2 1.8 compare_and_fusion.3
  95.1 0.5 bitcast_multiply_fusion.1
  95.6 1.0 fusion.22
  96.6 1.7 convolution_convert_fusion
  98.6 1.7 fusion.20
  100.5 0.8 copy-done.7
  101.7 0.8 slice.68
  103.3 26.4 %all_gather.39 = bf16[512,512]{0,1:T(8,128)(2,1)} all-gather(bf16[128,512]{0,1:T(8,128)(2,1)S(1)} %pad_maximum_fusion.1), channel_id=1, replica_groups=mesh['group'=2,'context'=4,'head'=4] {'context'}, dimensions={0}, use_global_device_ids=true | all-gather | bytes 655360 | tf_op jit(solution)/shard_map/all_gather | solution.py:24
  130.0 15.0 %all_gather.37 = bf16[8,64,256]{2,1,0:T(8,128)(2,1)} all-gather(bf16[2,64,256]{2,1,0:T(8,128)(2,1)S(1)} %constant_dynamic-slice_fusion.3), channel_id=1, replica_groups=mesh['group'=2,'context'=4,'head'=4] {'context'}, dimensions={0}, use_global_device_ids=true | all-gather | bytes 327680 | tf_op jit(solution)/shard_map/all_gather | solution.py:258
  145.2 0.7 add.226
  146.0 0.7 eq.150
  146.7 16.1 %all_gather.38 = bf16[8,64,256]{2,1,0:T(8,128)(2,1)S(1)} all-gather(bf16[2,64,256]{2,1,0:T(8,128)(2,1)S(1)} %constant_dynamic-slice_fusion.2), channel_id=1, replica_groups=mesh['group'=2,'context'=4,'head'=4] {'context'}, dimensions={0}, use_global_device_ids=true | all-gather | bytes 327680 | tf_op jit(solution)/shard_map/all_gather | solution.py:259
  163.1 1.0 copy.166
  164.2 0.8 multiply_reduce_fusion.2
  165.9 0.5 copy-done.22
  166.7 0.5 fusion.74
  167.1 0.5 copy-done.4
  167.6 0.5 fusion.73
  168.1 0.4 fusion.28
  168.5 0.3 fusion.26
  168.8 0.6 copy-done.36
  169.5 0.6 dynamic-slice
  170.1 0.4 fusion.18
  170.4 0.7 copy-done.3
  171.1 0.4 fusion.19
  171.5 0.8 dynamic-update-slice
  172.3 8.7 %all-reduce = bf16[4]{0:T(256)(128)(2,1)} all-reduce(bf16[4]{0:T(256)(128)(2,1)S(1)} %dynamic-update-slice), channel_id=1, replica_groups=mesh['group'=2,'context'=4,'head'=4] {'context'}, use_global_device_ids=true, to_apply=%add | all-reduce | flops 4 | bytes 16
  181.2 0.9 copy.169
  182.3 0.9 copy-done.13
  183.2 0.9 copy-done.9
  184.5 15.1 %all_gather.36 = bf16[2,8,128,128]{3,2,0,1:T(8,128)(2,1)S(1)} all-gather(bf16[2,8,32,128]{3,2,0,1:T(8,128)(2,1)S(1)} %copy.150), channel_id=1, replica_groups=mesh['group'=2,'context'=4,'head'=4] {'context'}, dimensions={2}, use_global_device_ids=true | all-gather | bytes 655360 | tf_op jit(solution)/shard_map/all_gather | solution.py:224
  199.7 0.5 compare_convert_fusion
  200.2 0.6 copy-done.15
  200.9 1.2 convolution_multiply_fusion.3
  202.1 1.5 fusion.43
  203.5 0.7 convolution_subtract_fusion.1
  204.4 0.6 copy-done.37
  204.9 11.2 %while.14 = (s32[]{:T(128)}, f32[8,128,128]{1,2,0:T(8,128)S(1)}, f32[8,128,128]{1,2,0:T(8,128)S(1)}, s32[]{:T(128)}, bf16[4]{0:T(256)(128)(2,1)S(1)}, /*index=5*...) while((s32[]{:T(128)}, f32[8,128,128]{1,2,0:T(8,128)S(1)}, ...), condition=%wide.region_6.7_spmd, body=%wide.region_5.6_spmd.sunk | while | flops 403308544 | bytes 7340196 | solution.py:49
  204.9 1.1 constant_dynamic-slice_fusion.7
  206.2 0.6 dynamic_slice.39
  207.5 0.5 fusion.104
  208.2 0.5 fusion.103
  208.7 1.1 constant_dynamic-slice_fusion.7
  209.9 0.6 dynamic_slice.39
  211.2 0.5 fusion.104
  211.9 0.5 fusion.103
  212.4 1.1 constant_dynamic-slice_fusion.7
  213.7 0.6 dynamic_slice.39
  215.0 0.5 fusion.104
  215.7 0.5 fusion.103
  216.2 0.6 copy-done.26
  216.8 0.7 fusion.21
  217.5 0.3 convolution_bitcast_fusion.2
  217.9 0.7 copy-done.1
  218.6 0.8 multiply_reduce_fusion
  219.4 0.6 copy-done.29
  220.5 0.9 copy.168
  (148 shorter events, 7.8 us)
Async XLA Ops:
  7.2 122.8 %copy-start = (bf16[2,64,512]{2,1,0:T(8,128)(2,1)S(1)}, bf16[2,64,512]{2,1,0:T(8,128)(2,1)}, u32[]{:S(2)}) copy-start(bf16[2,64,512]{2,1,0:T(8,128)(2,1)} %param.32) | copy-start | bytes 393220
  7.2 197.1 %all-gather.7.cloned.1.call-start = ((), (), s32[]{:S(2)}) async-start(), calls=%async_computation.1 | async-start | bytes 1310720 | tf_op jit(solution)/shard_map/all_gather | solution.py:33
  7.2 4.0 %copy-start.11 = (bf16[128,512]{1,0:T(8,128)(2,1)S(1)}, bf16[128,512]{1,0:T(8,128)(2,1)}, u32[]{:S(2)}) copy-start(bf16[128,512]{1,0:T(8,128)(2,1)} %param.21) | copy-start | bytes 393220
  7.3 0.7 copy-start.34
  8.3 0.7 copy-start.31
  8.3 0.7 copy-start.32
  9.6 93.2 %copy-start.24 = (s32[128]{0:T(128)}, s32[128]{0:T(128)S(1)}, u32[]{:S(2)}) copy-start(s32[128]{0:T(128)S(1)} %get-tuple-element.106) | copy-start | bytes 1540
  9.6 1.2 copy-start.33
  11.0 84.0 %copy-start.14 = (f32[8,128]{1,0:T(8,128)}, f32[8,128]{1,0:T(8,128)S(1)}, u32[]{:S(2)}) copy-start(f32[8,128]{1,0:T(8,128)S(1)} %convolution_bitcast_fusion.3) | copy-start | bytes 12292
  11.8 0.7 copy-start.21
  11.8 1.0 copy-start.6
  95.1 3.4 %copy-start.16 = (f32[8,128]{1,0:T(8,128)}, f32[8,128]{1,0:T(8,128)S(1)}, u32[]{:S(2)}) copy-start(f32[8,128]{1,0:T(8,128)S(1)} %get-tuple-element.135) | copy-start | bytes 12292
  98.4 105.9 %all-gather.5.cloned.1.call-start = ((), (), s32[]{:S(2)}) async-start(), calls=%async_computation | async-start | bytes 1310720 | tf_op jit(solution)/shard_map/all_gather | solution.py:33
  100.3 0.9 copy-start.7
  101.7 0.9 copy-start.19
  101.7 1.0 copy-start.20
  130.0 15.0 %copy-start.35 = (s32[8]{0:T(128)S(1)}, s32[8]{0:T(128)}, u32[]{:S(2)}) copy-start(s32[8]{0:T(128)} %param.37) | copy-start | bytes 100
  130.0 16.6 %copy-start.18 = (bf16[2,64,512]{2,1,0:T(8,128)(2,1)S(1)}, bf16[2,64,512]{2,1,0:T(8,128)(2,1)}, u32[]{:S(2)}) copy-start(bf16[2,64,512]{2,1,0:T(8,128)(2,1)} %param.33) | copy-start | bytes 393220
  145.0 17.7 %copy-start.8 = (bf16[128,1024]{1,0:T(8,128)(2,1)S(1)}, bf16[128,1024]{1,0:T(8,128)(2,1)}, u32[]{:S(2)}) copy-start(bf16[128,1024]{1,0:T(8,128)(2,1)} %param.29) | copy-start | bytes 786436
  163.1 1.0 copy-start.12
  165.0 1.6 copy-start.2
  165.7 0.7 copy-start.22
  165.7 0.7 copy-start.23
  165.7 1.0 copy-start.10
  165.8 0.6 copy-start.25
  165.8 0.7 copy-start.27
  166.7 0.9 copy-start.4
  168.8 0.7 copy-start.36
  170.0 1.0 copy-start.3
  171.1 1.2 copy-start.5
  182.3 0.9 copy-start.13
  183.2 0.9 copy-start.9
  184.5 15.2 %copy-start.28 = (s32[128]{0:T(128)S(1)}, s32[128]{0:T(128)}, u32[]{:S(2)}) copy-start(s32[128]{0:T(128)} %get-tuple-element.108) | copy-start | bytes 1540
  200.2 0.7 copy-start.15
  202.1 1.5 copy-start.17
  204.3 0.6 copy-start.37
  216.2 0.7 copy-start.26
  216.8 0.7 copy-start.30
  217.5 1.0 copy-start.1
  219.4 0.7 copy-start.29
Sparse Core Ops, SparseCore 0:
  98.5 34.6 all-gather.6
  135.3 31.6 all-gather.4
